TPU v7x, 512 devices: a whole 4x8x8 slice. The times are simulated.
512 devices in a mesh: dp: 64 (over y, z), fsdp: 8 (over x, core).
Axes of the slice: x: 4, y: 8, z: 8, core: 2. Of those that a mesh axis runs over, the one named last changes fastest.
Arguments:
- frames: bfloat16 [524288, 512], P(('dp', 'fsdp')), may hold values from -6 to 6
- utt_pairs: int32 [8, 64, 4], P('fsdp'), may hold values from 32 to 256, as said below
- utt_dest: int32 [8, 64, 4], P('fsdp'), may hold values from 0 to 63, as said below
- conv_weight: bfloat16 [1536, 512], P('dp'), may hold values from -0.15625 to 0.15625
- proj_weight: bfloat16 [512, 1536], P('dp'), may hold values from -0.25 to 0.25
- point_weight: bfloat16 [2, 1536, 1536], P(None, None, 'fsdp'), may hold values from -0.15625 to 0.15625
- depth_weight: float32 [31, 1536], replicated, may hold values from -1 to 1
- gain_first: float32 [1536], replicated, may hold values from 0.5 to 1.5
- gain_second: float32 [1536], replicated, may hold values from 0.5 to 1.5
Outputs:
- encoded: bfloat16 [262144, 1536], P(('dp', 'fsdp'))
Inputs may be any that keep to these rules, and one draw needn't show every extreme that they name: `utt_pairs`: every loader holds exactly 512 pairs and every sequence device receives exactly 512 pairs, from 4 different loaders. Each loader holds one utterance of exactly 256 pairs and one of exactly 32 pairs. `utt_dest`: the 4 utterances of loader i go to the 4 different sequence devices (i + k * 64 / 4) mod 64, k = 0 .. 3, in some order.
All inputs are finite; a program needn't handle non-finite values.
Results may differ from a plain program's by a relative error of at most 0.012.
Values may be sent and summed in bfloat16 or wider, within the bound.
No kernel may reach another device: no remote copies, remote signals or barrier semaphores. Data moves between devices by JAX's collectives and lax.ppermute only.
A program may use at most 64 MiB of HBM per device.

v0:
```python
import jax
import jax.numpy as jnp
from jax import lax
from jax.sharding import PartitionSpec as P


def passed_along(value, axis, steps):
    count = lax.axis_size(axis)
    pairs = [(source, (source + steps) % count) for source in range(count)]
    return lax.ppermute(value, axis, pairs)


def frontend(pair_rows, first_rows, conv_full):
    channels = pair_rows.shape[1] // 2
    even_frames = pair_rows[:, :channels]
    odd_frames = pair_rows[:, channels:]
    earlier = jnp.pad(odd_frames[:-1], ((1, 0), (0, 0)))
    earlier = jnp.where(first_rows[:, None], jnp.zeros_like(earlier), earlier)
    summed = jnp.dot(earlier, conv_full[:channels], preferred_element_type=jnp.float32)
    summed = summed + jnp.dot(
        even_frames, conv_full[channels : 2 * channels], preferred_element_type=jnp.float32
    )
    summed = summed + jnp.dot(
        odd_frames, conv_full[2 * channels :], preferred_element_type=jnp.float32
    )
    return jax.nn.relu(summed).astype(jnp.bfloat16)


def layer_norm(values, scales):
    centered = values - jnp.mean(values, axis=-1, keepdims=True)
    variance = jnp.mean(centered * centered, axis=-1, keepdims=True)
    return centered * lax.rsqrt(variance + 1e-05) * scales


def depthwise(gated, depth_weight, positions, lengths):
    row_count = gated.shape[0]
    kernel_size = depth_weight.shape[0]
    half_width = kernel_size // 2
    padded = jnp.pad(gated.astype(jnp.float32), ((half_width, half_width), (0, 0)))
    mixed = jnp.zeros(gated.shape, jnp.float32)
    for tap_index in range(kernel_size):
        offset = tap_index - half_width
        inside = (positions + offset >= 0) & (positions + offset < lengths)
        term = padded[tap_index : tap_index + row_count] * depth_weight[tap_index][None, :]
        mixed = mixed + jnp.where(inside[:, None], term, jnp.zeros_like(term))
    return mixed


def gate_product(normed, value_weight, gate_weight):
    value_part = jnp.dot(normed, value_weight, preferred_element_type=jnp.float32)
    gate_part = jnp.dot(normed, gate_weight, preferred_element_type=jnp.float32)
    return (value_part * jax.nn.sigmoid(gate_part)).astype(jnp.bfloat16)


def cut_pieces(source_rows, own_starts, slot_size, utt_count):
    padded = jnp.pad(source_rows, ((0, slot_size), (0, 0)))
    pieces = []
    for slot_index in range(utt_count):
        pieces.append(lax.dynamic_slice_in_dim(padded, own_starts[slot_index], slot_size, 0))
    return pieces


def body(
    frames,
    utt_pairs,
    utt_dest,
    conv_weight,
    proj_weight,
    point_weight,
    depth_weight,
    gain_first,
    gain_second,
):
    node_count = lax.axis_size("dp")
    own_index = lax.axis_index("dp")
    pair_count = frames.shape[0] // 2
    channels = frames.shape[1]
    utt_count = utt_pairs.shape[2]
    spacing = node_count // utt_count
    slot_size = pair_count // 2
    pair_table = utt_pairs[0]
    dest_table = utt_dest[0]
    loader_ids = jnp.arange(node_count, dtype=jnp.int32)
    slot_ids = jnp.arange(utt_count, dtype=jnp.int32)
    slot_table = (dest_table - loader_ids[:, None]) % node_count // spacing
    matches = (slot_table[:, :, None] == slot_ids[None, None, :]).astype(jnp.int32)
    loader_offsets = jnp.cumsum(pair_table, axis=1) - pair_table
    slot_counts = jnp.sum(matches * pair_table[:, :, None], axis=1)
    slot_starts = jnp.sum(matches * loader_offsets[:, :, None], axis=1)
    conv_full, proj_full = (
        lax.all_gather(conv_weight, "dp", axis=0, tiled=True),
        lax.all_gather(proj_weight, "dp", axis=0, tiled=True),
    )
    own_starts = slot_starts[own_index]
    sources = (own_index - slot_ids * spacing) % node_count
    piece_lengths = slot_counts[sources, slot_ids]
    earlier_pieces = (sources[None, :] < sources[:, None]).astype(jnp.int32)
    piece_offsets = jnp.sum(earlier_pieces * piece_lengths[None, :], axis=1)
    pair_rows = jnp.arange(pair_count, dtype=jnp.int32)
    inside = (
        (pair_rows[:, None] >= piece_offsets[None, :])
        & (pair_rows[:, None] < piece_offsets[None, :] + piece_lengths[None, :])
    ).astype(jnp.int32)
    piece_index = jnp.sum(inside * slot_ids[None, :], axis=1)
    positions = pair_rows - jnp.sum(inside * piece_offsets[None, :], axis=1)
    lengths = jnp.sum(inside * piece_lengths[None, :], axis=1)
    flat_slot = piece_index * slot_size + positions
    frame_pairs = frames.reshape(pair_count, 2 * channels)
    pieces = cut_pieces(frame_pairs, own_starts, slot_size, utt_count)
    arrived = [pieces[0]]
    for slot_index in range(1, utt_count):
        arrived.append(passed_along(pieces[slot_index], "dp", slot_index * spacing))
    stacked = jnp.concatenate(arrived, axis=0)
    packed = jnp.take(stacked, flat_slot, axis=0)
    front = frontend(packed, positions == 0, conv_full)
    projected = jnp.dot(front, proj_full, preferred_element_type=jnp.float32).astype(jnp.bfloat16)
    normed = layer_norm(projected.astype(jnp.float32), gain_first).astype(jnp.bfloat16)
    weight_part = lax.all_gather(point_weight, "fsdp", axis=2, tiled=True)
    gated = gate_product(normed, weight_part[0], weight_part[1])
    mixed = depthwise(gated, depth_weight, positions, lengths)
    scaled = layer_norm(mixed, gain_second)
    return (scaled * jax.nn.sigmoid(scaled)).astype(jnp.bfloat16)


def solution(mesh):
    in_specs = (
        P(("dp", "fsdp"), None),
        P("fsdp", None, None),
        P("fsdp", None, None),
        P("dp", None),
        P("dp", None),
        P(None, None, "fsdp"),
        P(),
        P(),
        P(),
    )
    out_specs = P(("dp", "fsdp"), None)
    return jax.shard_map(body, mesh=mesh, in_specs=in_specs, out_specs=out_specs, check_vma=False)
```

profile of v0, /device:TPU:1, one launch (start us, length us, event | category | flops | bytes accessed | tf_op | source)
XLA Modules:
  0.0 303.4 jit_solution(6321874885541037050)
XLA Ops:
  6.5 0.7 all-gather.4.cloned.1.call-update
  7.3 0.0 all-gather.6.cloned.1.call-start
  7.3 0.7 all-gather.6.cloned.1.call-update
  8.0 0.0 all-gather.8.cloned.1.call-start
  8.1 0.7 all-gather.8.cloned.1.call-update
  8.8 0.8 reduce_window_sum.11
  9.5 0.7 add_select_fusion
  10.2 0.7 select_reduce_fusion.4
  10.9 0.1 constant_dynamic-slice_fusion
  11.0 0.6 fusion.84
  16.7 1.4 reshape.518
  20.7 1.6 pad_dynamic-slice_fusion.3
  22.2 5.1 %collective-permute-start = (bf16[256,1024]{1,0:T(8,128)(2,1)S(1)}, bf16[256,1024]{1,0:T(8,128)(2,1)S(1)}, u32[]{:S(2)}, u32[]{:S(2)}) collective-permute-start(bf16[256,1024]{1,0:T(8,128)(2,1)S(1)} %get-tuple-element.44), channel_id=1, source_target_pairs={{0,128},{8,136},{16,144},{24,152},{32,160},{40,168},{48,176},{56,1... | collective-permute-start | bytes 1572872 | tf_op jit(solution)/shard_map/ppermute | solution.py:10
  27.3 5.7 %collective-permute-start.1 = (bf16[256,1024]{1,0:T(8,128)(2,1)S(1)}, bf16[256,1024]{1,0:T(8,128)(2,1)}, u32[]{:S(2)}, u32[]{:S(2)}) collective-permute-start(bf16[256,1024]{1,0:T(8,128)(2,1)S(1)} %get-tuple-element.45), channel_id=1, source_target_pairs={{0,256},{8,264},{16,272},{24,280},{32,288},{40,296},{48,304},{56,3... | collective-permute-start | bytes 1572872 | tf_op jit(solution)/shard_map/ppermute | solution.py:10
  33.0 5.0 %collective-permute-start.2 = (bf16[256,1024]{1,0:T(8,128)(2,1)S(1)}, bf16[256,1024]{1,0:T(8,128)(2,1)}, u32[]{:S(2)}, u32[]{:S(2)}) collective-permute-start(bf16[256,1024]{1,0:T(8,128)(2,1)S(1)} %get-tuple-element.46), channel_id=1, source_target_pairs={{0,384},{8,392},{16,400},{24,408},{32,416},{40,424},{48,432},{56,4... | collective-permute-start | bytes 1572872 | tf_op jit(solution)/shard_map/ppermute | solution.py:10
  38.0 0.6 gather_fusion
  38.6 0.2 select_reduce_fusion.5
  38.8 0.1 select_reduce_fusion.2
  39.0 0.0 copy-done.1
  39.0 0.8 slice_reduce_fusion.29
  39.8 0.3 slice_reduce_fusion.30
  40.1 0.1 compare_and_fusion.31
  40.2 1.1 collective-permute-done
  41.2 27.6 %collective-permute-done.1 = bf16[256,1024]{1,0:T(8,128)(2,1)} collective-permute-done((bf16[256,1024]{1,0:T(8,128)(2,1)S(1)}, bf16[256,1024]{1,0:T(8,128)(2,1)}, u32[]{:S(2)}, u32[]{:S(2)}) %collective-permute-start.1) | collective-permute-done | bytes 524320 | tf_op jit(solution)/shard_map/ppermute | solution.py:10
  68.8 11.9 %collective-permute-done.2 = bf16[256,1024]{1,0:T(8,128)(2,1)} collective-permute-done((bf16[256,1024]{1,0:T(8,128)(2,1)S(1)}, bf16[256,1024]{1,0:T(8,128)(2,1)}, u32[]{:S(2)}, u32[]{:S(2)}) %collective-permute-start.2) | collective-permute-done | bytes 524320 | tf_op jit(solution)/shard_map/ppermute | solution.py:10
  80.7 1.5 pad_maximum_fusion
  82.3 2.2 gather_fusion.1
  84.5 0.2 broadcast_select_fusion
  84.7 31.2 %all-gather.4.cloned.1.call-done = bf16[1536,512]{1,0:T(8,128)(2,1)} async-done(((bf16[24,512]{1,0:T(8,128)(2,1)}), bf16[1536,512]{1,0:T(8,128)(2,1)}) %all-gather.4.cloned.1.call-update) | async-done | bytes 1572880 | tf_op jit(solution)/shard_map/all_gather | solution.py:91
  116.0 1.5 fusion.62
  117.5 2.5 convolution_add_fusion.1
  120.0 78.9 %all-gather.6.cloned.1.call-done = bf16[512,1536]{1,0:T(8,128)(2,1)} async-done(((bf16[8,1536]{1,0:T(8,128)(2,1)}), bf16[512,1536]{1,0:T(8,128)(2,1)}) %all-gather.6.cloned.1.call-update) | async-done | bytes 1572880 | tf_op jit(solution)/shard_map/all_gather | solution.py:92
  198.9 3.2 %convert_reduce_fusion = (f32[512]{0:T(512)S(1)}, bf16[512,1536]{1,0:T(8,128)(2,1)S(1)}) fusion(bf16[512,1536]{1,0:T(8,128)(2,1)} %all-gather.6.cloned.1.call-done, f32[512,512]{1,0:T(8,128)} %convolution_add_fusion.1, bf16[1536,512]{1,0:T(8,128)(2,1)} %all-gather.4.cloned.1.call-done, bf16[512,1024]{1,0:T(8,128)(2,1)S(1)} %broadcast_select_fusion), kind=kOutput, calls=%fused_computation.7 | convolution fusion | flops 1076887040 | bytes 5244928 | tf_op jit(solution)/shard_map/dot_general | solution.py:116
  202.1 0.6 fusion.8
  202.7 59.3 %all-gather.8.cloned.1.call-done = bf16[2,1536,1536]{1,2,0:T(8,128)(2,1)} async-done(((bf16[2,1536,192]{1,2,0:T(8,128)(2,1)}), bf16[2,1536,1536]{1,2,0:T(8,128)(2,1)}) %all-gather.8.cloned.1.call-update) | async-done | bytes 9437200 | tf_op jit(solution)/shard_map/all_gather | solution.py:118
  261.9 5.2 %fusion.7 = f32[512,1536]{1,0:T(8,128)S(1)} fusion(bf16[2,1536,1536]{1,2,0:T(8,128)(2,1)} %all-gather.8.cloned.1.call-done, bf16[512,1536]{1,0:T(8,128)(2,1)S(1)} %get-tuple-element.85, f32[1536]{0:T(1024)S(1)} %copy-done.10, f32[512]{0:T(512)S(1)} %add_rsqrt_fusion.1, f32[512]{0:T(512)S(1)} %broadcast_multiply_fusion.1), kind=kOutput, calls=%fused_computation.13 | convolution fusion | flops 2421424128 | bytes 9447424 | tf_op jit(solution)/shard_map/dot_general | solution.py:51
  267.2 2.7 fusion.53
  269.9 0.0 copy-done.2
  269.9 0.0 copy-done.3
  269.9 0.0 copy-done.4
  269.9 0.0 copy-done.5
  269.9 0.0 copy-done.6
  269.9 0.0 copy-done.7
  269.9 24.0 %fusion.83 = (f32[512]{0:T(512)S(1)}, f32[512,1536]{1,0:T(8,128)S(1)}) fusion(f32[1536]{0:T(1024)S(1)} %copy-done.6, pred[512]{0:T(512)(128)(4,1)S(1)} %get-tuple-element.48, f32[1536]{0:T(1024)S(1)} %copy-done.7, pred[512]{0:T(512)(128)(4,1)S(1)} %get-tuple-element.49, f32[1536]{0:T(1024)S(1)} %get-tuple-element.6, ...), kind=kLoop, calls=%fused_computation.211 | loop fusion | flops 73137664 | bytes 6499840 | tf_op jit(solution)/shard_map/reduce_sum | solution.py:30
  293.9 0.0 copy-start.8
  294.0 0.4 multiply_reduce_fusion
  294.4 0.2 copy-done.8
  294.6 2.2 multiply_convert_fusion
  (25 shorter events, 0.1 us)
Async XLA Ops:
  6.5 109.4 %all-gather.4.cloned.1.call-start = ((), (), s32[]{:S(2)}) async-start(), calls=%async_computation | async-start | bytes 1597440 | tf_op jit(solution)/shard_map/all_gather | solution.py:91
  7.3 191.6 %all-gather.6.cloned.1.call-start = ((), (), s32[]{:S(2)}) async-start(), calls=%async_computation.1 | async-start | bytes 1597440 | tf_op jit(solution)/shard_map/all_gather | solution.py:92
  8.0 253.9 %all-gather.8.cloned.1.call-start = ((), (), s32[]{:S(2)}) async-start(), calls=%async_computation.2 | async-start | bytes 10616832 | tf_op jit(solution)/shard_map/all_gather | solution.py:118
  8.7 30.2 %copy-start.1 = (f32[31,1536]{1,0:T(8,128)S(1)}, f32[31,1536]{1,0:T(8,128)}, u32[]{:S(2)}) copy-start(f32[31,1536]{1,0:T(8,128)} %param.15) | copy-start | bytes 571396
  22.2 19.0 %collective-permute-start = (bf16[256,1024]{1,0:T(8,128)(2,1)S(1)}, bf16[256,1024]{1,0:T(8,128)(2,1)S(1)}, u32[]{:S(2)}, u32[]{:S(2)}) collective-permute-start(bf16[256,1024]{1,0:T(8,128)(2,1)S(1)} %get-tuple-element.44), channel_id=1, source_target_pairs={{0,128},{8,136},{16,144},{24,152},{32,160},{40,168},{48,176},{56,1... | collective-permute-start | bytes 1572872 | tf_op jit(solution)/shard_map/ppermute | solution.py:10
  27.3 41.5 %collective-permute-start.1 = (bf16[256,1024]{1,0:T(8,128)(2,1)S(1)}, bf16[256,1024]{1,0:T(8,128)(2,1)}, u32[]{:S(2)}, u32[]{:S(2)}) collective-permute-start(bf16[256,1024]{1,0:T(8,128)(2,1)S(1)} %get-tuple-element.45), channel_id=1, source_target_pairs={{0,256},{8,264},{16,272},{24,280},{32,288},{40,296},{48,304},{56,3... | collective-permute-start | bytes 1572872 | tf_op jit(solution)/shard_map/ppermute | solution.py:10
  33.0 47.8 %collective-permute-start.2 = (bf16[256,1024]{1,0:T(8,128)(2,1)S(1)}, bf16[256,1024]{1,0:T(8,128)(2,1)}, u32[]{:S(2)}, u32[]{:S(2)}) collective-permute-start(bf16[256,1024]{1,0:T(8,128)(2,1)S(1)} %get-tuple-element.46), channel_id=1, source_target_pairs={{0,384},{8,392},{16,400},{24,408},{32,416},{40,424},{48,432},{56,4... | collective-permute-start | bytes 1572872 | tf_op jit(solution)/shard_map/ppermute | solution.py:10
  41.2 39.5 %copy-start = (bf16[256,1024]{1,0:T(8,128)(2,1)}, bf16[256,1024]{1,0:T(8,128)(2,1)S(1)}, u32[]{:S(2)}) copy-start(bf16[256,1024]{1,0:T(8,128)(2,1)S(1)} %collective-permute-done) | copy-start | bytes 1572868
  120.0 142.0 %copy-start.10 = (f32[1536]{0:T(1024)S(1)}, f32[1536]{0:T(1024)}, u32[]{:S(2)}) copy-start(f32[1536]{0:T(1024)} %param.16) | copy-start | bytes 18436
  261.9 5.2 %copy-start.9 = (bf16[2,1536,1536]{1,2,0:T(8,128)(2,1)S(1)}, bf16[2,1536,1536]{1,2,0:T(8,128)(2,1)}, u32[]{:S(2)}) copy-start(bf16[2,1536,1536]{1,2,0:T(8,128)(2,1)} %all-gather.8.cloned.1.call-done) | copy-start | bytes 28311556
  267.1 2.8 copy-start.2
  267.1 2.8 copy-start.3
  267.1 2.8 copy-start.4
  267.2 2.8 copy-start.5
  267.2 2.8 copy-start.6
  267.2 2.8 copy-start.7
  293.9 0.7 copy-start.8
Sparse Core Ops, SparseCore 0:
  10.4 105.5 all-gather.3
  119.0 79.7 all-gather.5
  201.0 60.9 all-gather.7
where the time goes:
time: 304 us; the launch traced here: 303 us
  waiting for transfers between devices  212 us (70%)
  other arithmetic  31.5 us (10%)
  between operations  21 us (7%)
  starting transfers between devices  15.8 us (5%)
  matrix products  15 us (5%)
  local copies, waits for them, and re-layouts  7.95 us (3%)
    all_gather x1, waiting for transfers between devices, body(): lax.all_gather(proj_weight, 'dp', axis=0, tiled=True)  78.9 us
    all_gather x1, waiting for transfers between devices, body(): weight_part = lax.all_gather(point_weight, 'fsdp', axis=2, tiled=True)  59.3 us
    ppermute x3, waiting for transfers between devices, passed_along(): return lax.ppermute(value, axis, pairs)  40.6 us
    all_gather x1, waiting for transfers between devices, body(): lax.all_gather(conv_weight, 'dp', axis=0, tiled=True)  31.2 us
    reduce_sum x1, other arithmetic, layer_norm(): centered = values - jnp.mean(values, axis=-1, keepdims=True)  24 us
    ppermute x3, starting transfers between devices, passed_along(): return lax.ppermute(value, axis, pairs)  15.7 us
  transfers between devices with their start and end apart: 6, of which 6 were waited for; matrix products, arithmetic and copies ran while one was open for 7% of the time, Pallas kernels for 0%

commit v1 on v0

--- a/solution.py
+++ b/solution.py
@@ -2,6 +2,12 @@
 import jax.numpy as jnp
 from jax import lax
 from jax.sharding import PartitionSpec as P
+
+
+def shifts_all_settle(mat, d0):
+    mat = jnp.moveaxis(mat, 0, d0)
+    e_now = mat.shape
+    return mat.reshape(*e_now[:d0], e_now[d0] * e_now[d0 + 1], *e_now[d0 + 2 :])
 
 
 def passed_along(value, axis, steps):
@@ -115,7 +121,21 @@
     front = frontend(packed, positions == 0, conv_full)
     projected = jnp.dot(front, proj_full, preferred_element_type=jnp.float32).astype(jnp.bfloat16)
     normed = layer_norm(projected.astype(jnp.float32), gain_first).astype(jnp.bfloat16)
-    weight_part = lax.all_gather(point_weight, "fsdp", axis=2, tiled=True)
+    devs = lax.axis_size("fsdp")
+    table = [(i, (i + 1) % devs) for i in range(devs)]
+    entries = [(at, b) for b, at in table]
+    small, block_out = ([], [])
+    for num in range(devs - 1):
+        if num % 2 == 0:
+            small.append(lax.ppermute(small[-1] if small else point_weight, "fsdp", table))
+        else:
+            block_out.append(
+                lax.ppermute(block_out[-1] if block_out else point_weight, "fsdp", entries)
+            )
+    raw_out = jnp.stack([*small[::-1], point_weight, *block_out])
+    frame_out = lax.axis_index("fsdp") - len(small)
+    raw_out = raw_out[(jnp.arange(devs) - frame_out) % devs]
+    weight_part = shifts_all_settle(raw_out, 2)
     gated = gate_product(normed, weight_part[0], weight_part[1])
     mixed = depthwise(gated, depth_weight, positions, lengths)
     scaled = layer_norm(mixed, gain_second)

time: 304 us -> 279 us (0.918); the launches traced: 303 us -> 275 us
  waiting for transfers between devices: 212 us -> 138 us
  local copies, waits for them, and re-layouts: 7.95 us -> 39.1 us
  starting transfers between devices: 15.8 us -> 28 us
    all_gather x1 -> x0, waiting for transfers between devices: 59.3 us -> none  [body(): weight_part = lax.all_gather(point_weight, 'fsdp', axis=2, tiled=True)]
    ppermute x3, waiting for transfers between devices: 40.6 us -> 16 us  [passed_along(): return lax.ppermute(value, axis, pairs)]
    ppermute x0 -> x7, starting transfers between devices: none -> 18.5 us  [the longest x4 13.5 us: body(): lax.ppermute(small[-1] if small else point_weight, 'fsdp', table)]
    unnamed x22 -> x37, local copies, waits for them, and re-layouts: 0.26 us -> 15.7 us
    ppermute x0 -> x7, waiting for transfers between devices: none -> 10.4 us  [the longest x4 10.3 us: body(): lax.ppermute(small[-1] if small else point_weight, 'fsdp', table)]
    gather x0 -> x1, local copies, waits for them, and re-layouts: none -> 9.02 us  [body(): raw_out = raw_out[(jnp.arange(devs) - frame_out) % devs]]
    all_gather x1, waiting for transfers between devices: 31.2 us -> 38.1 us  [body(): lax.all_gather(conv_weight, 'dp', axis=0, tiled=True)]
    ppermute x3, starting transfers between devices: 15.7 us -> 9.52 us  [passed_along(): return lax.ppermute(value, axis, pairs)]
  transfers between devices with their start and end apart: 6 -> 12, of which waited for: 6 -> 5; matrix products, arithmetic and copies ran while one was open for 7% -> 14% of each run, Pallas kernels for 0% -> 0%
where the time goes in v1:
time: 279 us; the launch traced here: 275 us
  waiting for transfers between devices  138 us (49%)
  local copies, waits for them, and re-layouts  39.1 us (14%)
  other arithmetic  34.2 us (12%)
  starting transfers between devices  28 us (10%)
  between operations  21.2 us (8%)
  matrix products  14.5 us (5%)
    all_gather x1, waiting for transfers between devices, body(): lax.all_gather(proj_weight, 'dp', axis=0, tiled=True)  73.1 us
    all_gather x1, waiting for transfers between devices, body(): lax.all_gather(conv_weight, 'dp', axis=0, tiled=True)  38.1 us
    reduce_sum x1, other arithmetic, layer_norm(): centered = values - jnp.mean(values, axis=-1, keepdims=True)  24.2 us
    ppermute x3, waiting for transfers between devices, passed_along(): return lax.ppermute(value, axis, pairs)  16 us
    unnamed x37, local copies, waits for them, and re-layouts  15.7 us
    ppermute x4, starting transfers between devices, body(): lax.ppermute(small[-1] if small else point_weight, 'fsdp', table)  13.5 us
    ppermute x4, waiting for transfers between devices, body(): lax.ppermute(small[-1] if small else point_weight, 'fsdp', table)  10.3 us
    ppermute x3, starting transfers between devices, passed_along(): return lax.ppermute(value, axis, pairs)  9.52 us
  transfers between devices with their start and end apart: 12, of which 5 were waited for; matrix products, arithmetic and copies ran while one was open for 14% of the time, Pallas kernels for 0%

profile of v1, /device:TPU:1, one launch (start us, length us, event | category | flops | bytes accessed | tf_op | source)
XLA Modules:
  0.0 275.3 jit_solution(2112608723777516423)
XLA Ops:
  6.5 0.7 all-gather.3.cloned.1.call-update
  7.3 2.6 collective-permute-start.3
  9.9 4.3 %collective-permute-start.7 = (bf16[2,1536,192]{1,2,0:T(8,128)(2,1)}, bf16[2,1536,192]{1,2,0:T(8,128)(2,1)}, u32[]{:S(2)}, u32[]{:S(2)}) collective-permute-start(bf16[2,1536,192]{1,2,0:T(8,128)(2,1)} %param.14), channel_id=1, source_target_pairs={{1,0},{2,1},{3,2},{4,3},{5,4},{6,5},{7,6},{0,7},{9,8},{10,9},{11,1... | collective-permute-start | bytes 3538952 | tf_op jit(solution)/shard_map/ppermute | solution.py:133
  14.3 0.7 reduce_window_sum.11
  15.0 0.7 add_select_fusion
  15.7 0.7 select_reduce_fusion.4
  16.5 0.6 fusion.84
  22.1 1.4 reshape.572
  26.0 1.6 pad_dynamic-slice_fusion.3
  27.6 1.9 collective-permute-start.2
  29.5 3.2 %collective-permute-start.1 = (bf16[256,1024]{1,0:T(8,128)(2,1)S(1)}, bf16[256,1024]{1,0:T(8,128)(2,1)S(1)}, u32[]{:S(2)}, u32[]{:S(2)}) collective-permute-start(bf16[256,1024]{1,0:T(8,128)(2,1)S(1)} %get-tuple-element.47), channel_id=1, source_target_pairs={{0,256},{8,264},{16,272},{24,280},{32,288},{40,296},{48,304},{56,3... | collective-permute-start | bytes 1572872 | tf_op jit(solution)/shard_map/ppermute | solution.py:16
  32.7 4.4 %collective-permute-start = (bf16[256,1024]{1,0:T(8,128)(2,1)S(1)}, bf16[256,1024]{1,0:T(8,128)(2,1)}, u32[]{:S(2)}, u32[]{:S(2)}) collective-permute-start(bf16[256,1024]{1,0:T(8,128)(2,1)S(1)} %get-tuple-element.46), channel_id=1, source_target_pairs={{0,128},{8,136},{16,144},{24,152},{32,160},{40,168},{48,176},{56,1... | collective-permute-start | bytes 1572872 | tf_op jit(solution)/shard_map/ppermute | solution.py:16
  37.1 2.6 collective-permute-start.4
  39.7 0.6 gather_fusion
  40.6 0.7 select_reduce_fusion.2
  41.4 0.8 slice_reduce_fusion.29
  42.2 0.6 pad_clamp_fusion
  42.8 10.3 %collective-permute-done.4 = bf16[2,1536,192]{1,2,0:T(8,128)(2,1)} collective-permute-done((bf16[2,1536,192]{1,2,0:T(8,128)(2,1)}, bf16[2,1536,192]{1,2,0:T(8,128)(2,1)}, u32[]{:S(2)}, u32[]{:S(2)}) %collective-permute-start.4) | collective-permute-done | bytes 1179680 | tf_op jit(solution)/shard_map/ppermute | solution.py:130
  53.2 2.5 collective-permute-start.5
  55.7 0.6 pad_clamp_fusion.1
  56.6 0.8 compare_and_fusion.31
  57.4 13.8 %collective-permute-done.2 = bf16[256,1024]{1,0:T(8,128)(2,1)S(1)} collective-permute-done((bf16[256,1024]{1,0:T(8,128)(2,1)S(1)}, bf16[256,1024]{1,0:T(8,128)(2,1)S(1)}, u32[]{:S(2)}, u32[]{:S(2)}) %collective-permute-start.2) | collective-permute-done | bytes 524320 | tf_op jit(solution)/shard_map/ppermute | solution.py:16
  71.1 2.2 collective-permute-done
  73.3 1.5 pad_maximum_fusion
  74.9 2.1 gather_fusion.1
  77.2 0.6 collective-permute-start.9
  77.7 38.1 %all-gather.3.cloned.1.call-done = bf16[1536,512]{1,0:T(8,128)(2,1)} async-done(((bf16[24,512]{1,0:T(8,128)(2,1)}), bf16[1536,512]{1,0:T(8,128)(2,1)}) %all-gather.3.cloned.1.call-update) | async-done | bytes 1572880 | tf_op jit(solution)/shard_map/all_gather | solution.py:97
  115.9 1.5 fusion.59
  117.4 5.8 %collective-permute-start.6 = (bf16[2,1536,192]{1,2,0:T(8,128)(2,1)}, bf16[2,1536,192]{1,2,0:T(8,128)(2,1)}, u32[]{:S(2)}, u32[]{:S(2)}) collective-permute-start(bf16[2,1536,192]{1,2,0:T(8,128)(2,1)} %collective-permute-done.5), channel_id=1, source_target_pairs={{0,1},{1,2},{2,3},{3,4},{4,5},{5,6},{6,7},{7,0},{8,9},{9,10},{10,1... | collective-permute-start | bytes 3538952 | tf_op jit(solution)/shard_map/ppermute | solution.py:130
  123.2 2.4 convolution_add_fusion.1
  125.6 73.1 %all-gather.5.cloned.1.call-done = bf16[512,1536]{1,0:T(8,128)(2,1)} async-done(((bf16[8,1536]{1,0:T(8,128)(2,1)}), bf16[512,1536]{1,0:T(8,128)(2,1)}) %all-gather.5.cloned.1.call-update) | async-done | bytes 1572880 | tf_op jit(solution)/shard_map/all_gather | solution.py:98
  198.7 3.2 %convert_reduce_fusion = (f32[512]{0:T(512)S(1)}, bf16[512,1536]{1,0:T(8,128)(2,1)S(1)}) fusion(bf16[512,1536]{1,0:T(8,128)(2,1)} %all-gather.5.cloned.1.call-done, f32[512,512]{1,0:T(8,128)} %convolution_add_fusion.1, bf16[1536,512]{1,0:T(8,128)(2,1)} %all-gather.3.cloned.1.call-done, bf16[512,1024]{1,0:T(8,128)(2,1)S(1)} %broadcast_select_fusion), kind=kOutput, calls=%fused_computation.4 | convolution fusion | flops 1076887040 | bytes 5244928 | tf_op jit(solution)/shard_map/dot_general | solution.py:122
  202.0 0.5 fusion.5
  202.6 2.4 bitcast_dynamic-update-slice_fusion.7
  204.9 2.5 bitcast_dynamic-update-slice_fusion.6
  207.4 2.4 bitcast_dynamic-update-slice_fusion.5
  209.8 2.3 bitcast_dynamic-update-slice_fusion.4
  212.1 1.1 bitcast_dynamic-update-slice_fusion.3
  213.2 2.4 bitcast_dynamic-update-slice_fusion.2
  215.6 2.4 bitcast_dynamic-update-slice_fusion.1
  218.0 2.5 bitcast_dynamic-update-slice_fusion
  220.4 9.0 %gather_fusion.2 = bf16[8,2,1536,192]{2,3,1,0:T(8,128)(2,1)} fusion(bf16[8,2,1536,192]{2,3,1,0:T(8,128)(2,1)} %bitcast_dynamic-update-slice_fusion, s32[1024]{0:T(1024)} %pad_clamp_fusion), kind=kCustom, calls=%fused_computation.2 | custom fusion | bytes 18874400 | tf_op jit(solution)/shard_map/gather | solution.py:137
  229.5 4.4 %fusion.83 = (bf16[1,1536,8,192]{1,3,0,2:T(8,128)(2,1)S(1)}, bf16[1,1536,8,192]{1,3,0,2:T(8,128)(2,1)S(1)}) fusion(bf16[2,1536,8,192]{1,3,0,2:T(8,128)(2,1)} %bitcast.43), kind=kLoop, calls=%fused_computation.225 | loop fusion | bytes 18874368 | tf_op jit(solution)/shard_map/slice | solution.py:139
  233.9 4.6 %fusion.4 = f32[512,1536]{1,0:T(8,128)S(1)} fusion(bf16[1536,1536]{0,1:T(8,128)(2,1)S(1)} %bitcast.45, bf16[512,1536]{1,0:T(8,128)(2,1)} %copy-done, f32[1536]{0:T(1024)S(1)} %copy-done.14, f32[512]{0:T(512)S(1)} %add_rsqrt_fusion.1, f32[512]{0:T(512)S(1)} %broadcast_multiply_fusion.1), kind=kOutput, calls=%fused_computation.11 | convolution fusion | flops 2422210560 | bytes 9447424 | tf_op jit(solution)/shard_map/dot_general | solution.py:57
  238.5 2.8 fusion.50
  241.3 24.2 %fusion.82 = (f32[512]{0:T(512)S(1)}, f32[512,1536]{1,0:T(8,128)S(1)}) fusion(f32[1536]{0:T(1024)S(1)} %copy-done.10, pred[512]{0:T(512)(128)(4,1)S(1)} %get-tuple-element.50, f32[1536]{0:T(1024)S(1)} %copy-done.11, pred[512]{0:T(512)(128)(4,1)S(1)} %get-tuple-element.51, f32[1536]{0:T(1024)S(1)} %get-tuple-element.6, ...), kind=kLoop, calls=%fused_computation.224 | loop fusion | flops 73137664 | bytes 6499840 | tf_op jit(solution)/shard_map/reduce_sum | solution.py:36
  265.6 0.4 multiply_reduce_fusion
  266.3 2.2 multiply_convert_fusion
  (56 shorter events, 1.4 us)
Async XLA Ops:
  6.5 34.9 %copy-start.5 = (f32[31,1536]{1,0:T(8,128)S(1)}, f32[31,1536]{1,0:T(8,128)}, u32[]{:S(2)}) copy-start(f32[31,1536]{1,0:T(8,128)} %param.15) | copy-start | bytes 571396
  6.5 109.3 %all-gather.3.cloned.1.call-start = ((), (), s32[]{:S(2)}) async-start(), calls=%async_computation | async-start | bytes 1597440 | tf_op jit(solution)/shard_map/all_gather | solution.py:97
  7.3 191.5 %all-gather.5.cloned.1.call-start = ((), (), s32[]{:S(2)}) async-start(), calls=%async_computation.1 | async-start | bytes 1597440 | tf_op jit(solution)/shard_map/all_gather | solution.py:98
  7.3 29.8 %collective-permute-start.3 = (bf16[2,1536,192]{1,2,0:T(8,128)(2,1)}, bf16[2,1536,192]{1,2,0:T(8,128)(2,1)}, u32[]{:S(2)}, u32[]{:S(2)}) collective-permute-start(bf16[2,1536,192]{1,2,0:T(8,128)(2,1)} %param.14), channel_id=1, source_target_pairs={{0,1},{1,2},{2,3},{3,4},{4,5},{5,6},{6,7},{7,0},{8,9},{9,10},{10,1... | collective-permute-start | bytes 3538952 | tf_op jit(solution)/shard_map/ppermute | solution.py:130
  9.9 31.4 %collective-permute-start.7 = (bf16[2,1536,192]{1,2,0:T(8,128)(2,1)}, bf16[2,1536,192]{1,2,0:T(8,128)(2,1)}, u32[]{:S(2)}, u32[]{:S(2)}) collective-permute-start(bf16[2,1536,192]{1,2,0:T(8,128)(2,1)} %param.14), channel_id=1, source_target_pairs={{1,0},{2,1},{3,2},{4,3},{5,4},{6,5},{7,6},{0,7},{9,8},{10,9},{11,1... | collective-permute-start | bytes 3538952 | tf_op jit(solution)/shard_map/ppermute | solution.py:133
  27.6 43.6 %collective-permute-start.2 = (bf16[256,1024]{1,0:T(8,128)(2,1)S(1)}, bf16[256,1024]{1,0:T(8,128)(2,1)S(1)}, u32[]{:S(2)}, u32[]{:S(2)}) collective-permute-start(bf16[256,1024]{1,0:T(8,128)(2,1)S(1)} %get-tuple-element.48), channel_id=1, source_target_pairs={{0,384},{8,392},{16,400},{24,408},{32,416},{40,424},{48,432},{56,4... | collective-permute-start | bytes 1572872 | tf_op jit(solution)/shard_map/ppermute | solution.py:16
  29.5 41.6 %collective-permute-start.1 = (bf16[256,1024]{1,0:T(8,128)(2,1)S(1)}, bf16[256,1024]{1,0:T(8,128)(2,1)S(1)}, u32[]{:S(2)}, u32[]{:S(2)}) collective-permute-start(bf16[256,1024]{1,0:T(8,128)(2,1)S(1)} %get-tuple-element.47), channel_id=1, source_target_pairs={{0,256},{8,264},{16,272},{24,280},{32,288},{40,296},{48,304},{56,3... | collective-permute-start | bytes 1572872 | tf_op jit(solution)/shard_map/ppermute | solution.py:16
  32.7 40.6 %collective-permute-start = (bf16[256,1024]{1,0:T(8,128)(2,1)S(1)}, bf16[256,1024]{1,0:T(8,128)(2,1)}, u32[]{:S(2)}, u32[]{:S(2)}) collective-permute-start(bf16[256,1024]{1,0:T(8,128)(2,1)S(1)} %get-tuple-element.46), channel_id=1, source_target_pairs={{0,128},{8,136},{16,144},{24,152},{32,160},{40,168},{48,176},{56,1... | collective-permute-start | bytes 1572872 | tf_op jit(solution)/shard_map/ppermute | solution.py:16
  37.1 16.1 %collective-permute-start.4 = (bf16[2,1536,192]{1,2,0:T(8,128)(2,1)}, bf16[2,1536,192]{1,2,0:T(8,128)(2,1)}, u32[]{:S(2)}, u32[]{:S(2)}) collective-permute-start(bf16[2,1536,192]{1,2,0:T(8,128)(2,1)} %collective-permute-done.3), channel_id=1, source_target_pairs={{0,1},{1,2},{2,3},{3,4},{4,5},{5,6},{6,7},{7,0},{8,9},{9,10},{10,1... | collective-permute-start | bytes 3538952 | tf_op jit(solution)/shard_map/ppermute | solution.py:130
  41.3 35.9 %collective-permute-start.8 = (bf16[2,1536,192]{1,2,0:T(8,128)(2,1)}, bf16[2,1536,192]{1,2,0:T(8,128)(2,1)}, u32[]{:S(2)}, u32[]{:S(2)}) collective-permute-start(bf16[2,1536,192]{1,2,0:T(8,128)(2,1)} %collective-permute-done.7), channel_id=1, source_target_pairs={{1,0},{2,1},{3,2},{4,3},{5,4},{6,5},{7,6},{0,7},{9,8},{10,9},{11,1... | collective-permute-start | bytes 3538952 | tf_op jit(solution)/shard_map/ppermute | solution.py:133
  53.2 64.2 %collective-permute-start.5 = (bf16[2,1536,192]{1,2,0:T(8,128)(2,1)}, bf16[2,1536,192]{1,2,0:T(8,128)(2,1)}, u32[]{:S(2)}, u32[]{:S(2)}) collective-permute-start(bf16[2,1536,192]{1,2,0:T(8,128)(2,1)} %collective-permute-done.4), channel_id=1, source_target_pairs={{0,1},{1,2},{2,3},{3,4},{4,5},{5,6},{6,7},{7,0},{8,9},{9,10},{10,1... | collective-permute-start | bytes 3538952 | tf_op jit(solution)/shard_map/ppermute | solution.py:130
  56.6 18.3 %copy-start.12 = (s32[1024]{0:T(1024)S(1)}, s32[1024]{0:T(1024)}, u32[]{:S(2)}) copy-start(s32[1024]{0:T(1024)} %pad_clamp_fusion.1) | copy-start | bytes 12292
  71.1 2.2 copy-start.3
  71.1 2.2 copy-start.4
  77.2 140.8 %collective-permute-start.9 = (bf16[2,1536,192]{1,2,0:T(8,128)(2,1)}, bf16[2,1536,192]{1,2,0:T(8,128)(2,1)}, u32[]{:S(2)}, u32[]{:S(2)}) collective-permute-start(bf16[2,1536,192]{1,2,0:T(8,128)(2,1)} %collective-permute-done.8), channel_id=1, source_target_pairs={{1,0},{2,1},{3,2},{4,3},{5,4},{6,5},{7,6},{0,7},{9,8},{10,9},{11,1... | collective-permute-start | bytes 3538952 | tf_op jit(solution)/shard_map/ppermute | solution.py:133
  117.4 85.2 %collective-permute-start.6 = (bf16[2,1536,192]{1,2,0:T(8,128)(2,1)}, bf16[2,1536,192]{1,2,0:T(8,128)(2,1)}, u32[]{:S(2)}, u32[]{:S(2)}) collective-permute-start(bf16[2,1536,192]{1,2,0:T(8,128)(2,1)} %collective-permute-done.5), channel_id=1, source_target_pairs={{0,1},{1,2},{2,3},{3,4},{4,5},{5,6},{6,7},{7,0},{8,9},{9,10},{10,1... | collective-permute-start | bytes 3538952 | tf_op jit(solution)/shard_map/ppermute | solution.py:130
  202.0 18.5 %copy-start = (bf16[512,1536]{1,0:T(8,128)(2,1)}, bf16[512,1536]{1,0:T(8,128)(2,1)S(1)}, u32[]{:S(2)}) copy-start(bf16[512,1536]{1,0:T(8,128)(2,1)S(1)} %get-tuple-element.87) | copy-start | bytes 4718596
  204.9 7.2 %copy-start.2 = (bf16[2,1536,192]{1,2,0:T(8,128)(2,1)S(1)}, bf16[2,1536,192]{1,2,0:T(8,128)(2,1)}, u32[]{:S(2)}) copy-start(bf16[2,1536,192]{1,2,0:T(8,128)(2,1)} %param.14) | copy-start | bytes 3538948
  229.5 4.4 %copy-start.14 = (f32[1536]{0:T(1024)S(1)}, f32[1536]{0:T(1024)}, u32[]{:S(2)}) copy-start(f32[1536]{0:T(1024)} %param.16) | copy-start | bytes 18436
  233.9 4.6 %copy-start.1 = (bf16[512,1536]{1,0:T(8,128)(2,1)S(1)}, bf16[512,1536]{1,0:T(8,128)(2,1)}, u32[]{:S(2)}) copy-start(bf16[512,1536]{1,0:T(8,128)(2,1)} %copy-done) | copy-start | bytes 4718596
  238.5 2.8 %copy-start.6 = (f32[1536]{0:T(1024)S(1)}, f32[1536]{0:T(1024)}, u32[]{:S(2)}) copy-start(f32[1536]{0:T(1024)} %get-tuple-element.30) | copy-start | bytes 18436
  238.5 2.8 %copy-start.7 = (f32[1536]{0:T(1024)S(1)}, f32[1536]{0:T(1024)}, u32[]{:S(2)}) copy-start(f32[1536]{0:T(1024)} %get-tuple-element.31) | copy-start | bytes 18436
  238.5 2.8 %copy-start.8 = (f32[1536]{0:T(1024)S(1)}, f32[1536]{0:T(1024)}, u32[]{:S(2)}) copy-start(f32[1536]{0:T(1024)} %get-tuple-element.32) | copy-start | bytes 18436
  238.5 2.8 %copy-start.9 = (f32[1536]{0:T(1024)S(1)}, f32[1536]{0:T(1024)}, u32[]{:S(2)}) copy-start(f32[1536]{0:T(1024)} %get-tuple-element.33) | copy-start | bytes 18436
  238.5 2.8 %copy-start.10 = (f32[1536]{0:T(1024)S(1)}, f32[1536]{0:T(1024)}, u32[]{:S(2)}) copy-start(f32[1536]{0:T(1024)} %get-tuple-element.34) | copy-start | bytes 18436
  238.5 2.8 %copy-start.11 = (f32[1536]{0:T(1024)S(1)}, f32[1536]{0:T(1024)}, u32[]{:S(2)}) copy-start(f32[1536]{0:T(1024)} %get-tuple-element.35) | copy-start | bytes 18436
  265.6 0.7 copy-start.13
Sparse Core Ops, SparseCore 0:
  10.4 105.3 all-gather.2
  118.9 79.7 all-gather.4
